TPU v7x, 32 devices: a whole 2x2x4 slice. The times are simulated.
32 devices in a mesh: seq: 4 (over z), shard: 8 (over y, x, core).
Axes of the slice: x: 2, y: 2, z: 4, core: 2. Of those that a mesh axis runs over, the one named last changes fastest.
Arguments:
- frames: bfloat16 [8, 1024, 1536], P('shard', 'seq'), may hold values from -6 to 6
- text_states: bfloat16 [8, 64, 1536], P('shard'), may hold values from -6 to 6
- norm_gain: bfloat16 [3, 1536], P(None, 'shard'), may hold values from 0.5 to 1.5
- norm_bias: bfloat16 [3, 1536], P(None, 'shard'), may hold values from -3 to 3
- self_project: bfloat16 [3, 1536, 1536], P(None, 'shard'), may hold values from -0.15625 to 0.15625
- self_output: bfloat16 [1536, 1536], P('shard'), may hold values from -1.75 to 1.75
- cross_project: bfloat16 [3, 1536, 1536], P(None, 'shard'), may hold values from -0.15625 to 0.15625
- cross_output: bfloat16 [1536, 1536], P('shard'), may hold values from -0.625 to 0.625
- up_weight: bfloat16 [1536, 6144], P('shard'), may hold values from -0.15625 to 0.15625
- down_weight: bfloat16 [6144, 1536], P('shard'), may hold values from -0.078125 to 0.078125
- cotangent: bfloat16 [8, 1024, 1536], P('shard', 'seq'), may hold values from -6 to 6
Outputs:
- output: bfloat16 [8, 1024, 1536], P('shard', 'seq')
- frames_grad: float32 [8, 1024, 1536], P('shard', 'seq')
- text_grad: float32 [8, 64, 1536], P('shard')
- gain_grad: float32 [3, 1536], P(None, 'shard')
- bias_grad: float32 [3, 1536], P(None, 'shard')
- self_project_grad: float32 [3, 1536, 1536], P(None, 'shard')
- self_output_grad: float32 [1536, 1536], P('shard')
- cross_project_grad: float32 [3, 1536, 1536], P(None, 'shard')
- cross_output_grad: float32 [1536, 1536], P('shard')
- up_grad: float32 [1536, 6144], P('shard')
- down_grad: float32 [6144, 1536], P('shard')
All inputs are finite; a program needn't handle non-finite values.
Results may differ from a plain program's by a relative error of at most 0.022.
Values may be sent and summed in bfloat16 or wider, within the bound.
No kernel may reach another device: no remote copies, remote signals or barrier semaphores. Data moves between devices by JAX's collectives and lax.ppermute only.
A program may use at most 384 MiB of HBM per device.

v0:
```python
import jax
import jax.numpy as jnp
from jax import lax
from jax.sharding import PartitionSpec as P

HEAD_DIM = 64
QBLOCK = 512
EPSILON = 1e-05
MASKED_SCORE = -1e30


def layer_norm(hidden, gain, shift):
    center = hidden - jnp.mean(hidden, axis=-1, keepdims=True)
    spread = lax.rsqrt(jnp.mean(center * center, axis=-1, keepdims=True) + EPSILON)
    return center * spread * gain + shift


def exact_gelu(values):
    return jax.nn.gelu(values, approximate=False)


def contract(form, left, right):
    return jnp.einsum(form, left, right, preferred_element_type=jnp.float32)


def split_heads(values):
    return values.reshape(values.shape[:-1] + (values.shape[-1] // HEAD_DIM, HEAD_DIM))


def join_heads(values):
    return values.reshape(values.shape[:-2] + (values.shape[-2] * values.shape[-1],))


def causal_visible(start_row, row_count, stop_row):
    row_place = start_row + lax.broadcasted_iota(jnp.int32, (row_count, stop_row), 0)
    column_place = lax.broadcasted_iota(jnp.int32, (row_count, stop_row), 1)
    return column_place <= row_place


def block_scores(queries, key_rows, start_row, stop_row, scaling):
    scores = (
        contract("cqhe,ckhe->chqk", queries[:, start_row:stop_row], key_rows[:, :stop_row])
        * scaling
    )
    return jnp.where(
        causal_visible(start_row, stop_row - start_row, stop_row), scores, MASKED_SCORE
    )


def self_forward(queries, key_rows, value_rows, scaling):
    length = queries.shape[1]
    outputs = []
    totals = []
    for start_row in range(0, length, QBLOCK):
        stop_row = start_row + QBLOCK
        scores = block_scores(queries, key_rows, start_row, stop_row, scaling)
        largest = jnp.max(scores, axis=-1, keepdims=True)
        weights = jnp.exp(scores - largest)
        summed = jnp.sum(weights, axis=-1, keepdims=True)
        shares = (weights / summed).astype(jnp.bfloat16)
        outputs.append(contract("chqk,ckhe->cqhe", shares, value_rows[:, :stop_row]))
        totals.append(largest + jnp.log(summed))
    return (jnp.concatenate(outputs, axis=1), totals)


def self_backward(queries, key_rows, value_rows, totals, grad_out, scaling):
    length = queries.shape[1]
    grad_queries = []
    grad_keys = jnp.zeros(key_rows.shape, jnp.float32)
    grad_values = jnp.zeros(value_rows.shape, jnp.float32)
    for number, start_row in enumerate(range(0, length, QBLOCK)):
        stop_row = start_row + QBLOCK
        query_block = queries[:, start_row:stop_row]
        grad_block = grad_out[:, start_row:stop_row]
        scores = block_scores(queries, key_rows, start_row, stop_row, scaling)
        shares = jnp.exp(scores - totals[number])
        grad_shares = contract("cqhe,ckhe->chqk", grad_block, value_rows[:, :stop_row])
        centred = jnp.sum(shares * grad_shares, axis=-1, keepdims=True)
        grad_scores = (shares * (grad_shares - centred)).astype(jnp.bfloat16)
        grad_queries.append(
            contract("chqk,ckhe->cqhe", grad_scores, key_rows[:, :stop_row]) * scaling
        )
        grad_keys = grad_keys.at[:, :stop_row].add(
            contract("chqk,cqhe->ckhe", grad_scores, query_block) * scaling
        )
        grad_values = grad_values.at[:, :stop_row].add(
            contract("chqk,cqhe->ckhe", shares.astype(jnp.bfloat16), grad_block)
        )
    return (jnp.concatenate(grad_queries, axis=1), grad_keys, grad_values)


def cross_softmax(queries, key_rows, scaling):
    scores = contract("cfhe,cxhe->chxf", queries, key_rows) * scaling
    largest = jnp.max(scores, axis=2, keepdims=True)
    weights = jnp.exp(scores - largest)
    return weights / jnp.sum(weights, axis=2, keepdims=True)


def fetch_self(self_project, self_output, norm_gain, norm_bias):
    return (
        lax.all_gather(self_project, "shard", axis=1, tiled=True),
        lax.all_gather(self_output, "shard", axis=0, tiled=True),
        lax.all_gather(norm_gain, "shard", axis=1, tiled=True),
        lax.all_gather(norm_bias, "shard", axis=1, tiled=True),
    )


def fetch_cross(cross_project, cross_output):
    return (
        lax.all_gather(cross_project, "shard", axis=1, tiled=True),
        lax.all_gather(cross_output, "shard", axis=0, tiled=True),
    )


def fetch_mlp(up_weight, down_weight):
    return (
        lax.all_gather(up_weight, "shard", axis=0, tiled=True),
        lax.all_gather(down_weight, "shard", axis=0, tiled=True),
    )


def body(
    frames,
    text_states,
    norm_gain,
    norm_bias,
    self_project,
    self_output,
    cross_project,
    cross_output,
    up_weight,
    down_weight,
    cotangent,
):
    scaling = HEAD_DIM ** (-0.5)
    project_all, output_all, gain_all, bias_all = fetch_self(
        self_project, self_output, norm_gain, norm_bias
    )
    gains = gain_all.astype(jnp.float32)
    biases = bias_all.astype(jnp.float32)
    hidden = frames.astype(jnp.float32)
    normed_one, norm_pull_one = jax.vjp(layer_norm, hidden, gains[0], biases[0])
    inputs_one = normed_one.astype(jnp.bfloat16)
    projected = contract("cfd,jde->jcfe", inputs_one, project_all).astype(jnp.bfloat16)
    by_heads = lax.all_to_all(projected, "seq", split_axis=3, concat_axis=2, tiled=True)
    queries = split_heads(by_heads[0])
    key_rows = split_heads(by_heads[1])
    value_rows = split_heads(by_heads[2])
    attended_heads, totals = self_forward(queries, key_rows, value_rows, scaling)
    attended = lax.all_to_all(
        join_heads(attended_heads).astype(jnp.bfloat16),
        "seq",
        split_axis=1,
        concat_axis=2,
        tiled=True,
    )
    hidden_one = hidden + contract("cfd,de->cfe", attended, output_all)
    cross_all, cross_out_all = fetch_cross(cross_project, cross_output)
    normed_two, norm_pull_two = jax.vjp(layer_norm, hidden_one, gains[1], biases[1])
    inputs_two = normed_two.astype(jnp.bfloat16)
    cross_queries = contract("cfd,de->cfe", inputs_two, cross_all[0]).astype(jnp.bfloat16)
    cross_pairs = contract("cxd,jde->jcxe", text_states, cross_all[1:]).astype(jnp.bfloat16)
    text_keys = split_heads(cross_pairs[0])
    text_values = split_heads(cross_pairs[1])
    cross_shares = cross_softmax(split_heads(cross_queries), text_keys, scaling)
    cross_low = cross_shares.astype(jnp.bfloat16)
    mixed_text = join_heads(contract("chxf,cxhe->cfhe", cross_low, text_values)).astype(
        jnp.bfloat16
    )
    hidden_two = hidden_one + contract("cfd,de->cfe", mixed_text, cross_out_all)
    up_all, down_all = fetch_mlp(up_weight, down_weight)
    normed_three, norm_pull_three = jax.vjp(layer_norm, hidden_two, gains[2], biases[2])
    inputs_three = normed_three.astype(jnp.bfloat16)
    before_act = contract("cfd,dk->cfk", inputs_three, up_all)
    activated, gelu_pull = jax.vjp(exact_gelu, before_act)
    activated_low = activated.astype(jnp.bfloat16)
    result = hidden_two + contract("cfk,kd->cfd", activated_low, down_all)
    output = result.astype(jnp.bfloat16)
    up_all, down_all = fetch_mlp(up_weight, down_weight)
    grad_result = cotangent.astype(jnp.float32)
    grad_down = contract("cfk,cfd->kd", activated_low, cotangent)
    grad_act = contract("cfd,kd->cfk", cotangent, down_all)
    grad_before = gelu_pull(grad_act)[0].astype(jnp.bfloat16)
    grad_up = contract("cfd,cfk->dk", inputs_three, grad_before)
    grad_inputs_three = contract("cfk,dk->cfd", grad_before, up_all)
    grad_two_part, gain_three, bias_three = norm_pull_three(grad_inputs_three)
    grad_hidden_two = grad_result + grad_two_part
    up_share, down_share = (
        lax.psum_scatter(
            grad_up.astype(jnp.bfloat16), "shard", scatter_dimension=0, tiled=True
        ).astype(jnp.float32),
        lax.psum_scatter(
            grad_down.astype(jnp.bfloat16), "shard", scatter_dimension=0, tiled=True
        ).astype(jnp.float32),
    )
    cross_all, cross_out_all = fetch_cross(cross_project, cross_output)
    grad_low_two = grad_hidden_two.astype(jnp.bfloat16)
    grad_cross_out = contract("cfd,cfe->de", mixed_text, grad_low_two)
    grad_mixed = split_heads(
        contract("cfe,de->cfd", grad_low_two, cross_out_all).astype(jnp.bfloat16)
    )
    grad_shares = contract("cfhe,cxhe->chxf", grad_mixed, text_values)
    centred = jnp.sum(cross_shares * grad_shares, axis=2, keepdims=True)
    grad_scores = (cross_shares * (grad_shares - centred)).astype(jnp.bfloat16)
    grad_cross_query = join_heads(
        contract("chxf,cxhe->cfhe", grad_scores, text_keys) * scaling
    ).astype(jnp.bfloat16)
    grad_text_keys = join_heads(
        contract("chxf,cfhe->cxhe", grad_scores, split_heads(cross_queries)) * scaling
    )
    grad_text_values = join_heads(contract("chxf,cfhe->cxhe", cross_low, grad_mixed))
    grad_pairs = lax.psum(jnp.stack([grad_text_keys, grad_text_values]).astype(jnp.bfloat16), "seq")
    grad_text = contract("jcxe,jde->cxd", grad_pairs, cross_all[1:])
    grad_cross_pairs = contract("cxd,jcxe->jde", text_states, grad_pairs)
    grad_cross_first = contract("cfd,cfe->de", inputs_two, grad_cross_query)
    grad_inputs_two = contract("cfe,de->cfd", grad_cross_query, cross_all[0])
    grad_one_part, gain_two, bias_two = norm_pull_two(grad_inputs_two)
    grad_hidden_one = grad_hidden_two + grad_one_part
    cross_stack = jnp.concatenate([grad_cross_first[None], grad_cross_pairs], axis=0)
    cross_share, cross_out_share = (
        lax.psum_scatter(
            cross_stack.astype(jnp.bfloat16), "shard", scatter_dimension=1, tiled=True
        ).astype(jnp.float32),
        lax.psum_scatter(
            grad_cross_out.astype(jnp.bfloat16), "shard", scatter_dimension=0, tiled=True
        ).astype(jnp.float32),
    )
    project_all, output_all, gain_all, bias_all = fetch_self(
        self_project, self_output, norm_gain, norm_bias
    )
    grad_low_one = grad_hidden_one.astype(jnp.bfloat16)
    grad_self_out = contract("cfd,cfe->de", attended, grad_low_one)
    grad_attended = contract("cfe,de->cfd", grad_low_one, output_all).astype(jnp.bfloat16)
    grad_heads = lax.all_to_all(grad_attended, "seq", split_axis=2, concat_axis=1, tiled=True)
    grad_queries, grad_keys, grad_values = self_backward(
        queries, key_rows, value_rows, totals, split_heads(grad_heads), scaling
    )
    grad_stacked = jnp.stack(
        [join_heads(grad_queries), join_heads(grad_keys), join_heads(grad_values)]
    ).astype(jnp.bfloat16)
    grad_projected = lax.all_to_all(grad_stacked, "seq", split_axis=2, concat_axis=3, tiled=True)
    grad_self_project = contract("cfd,jcfe->jde", inputs_one, grad_projected)
    grad_inputs_one = contract("jcfe,jde->cfd", grad_projected, project_all)
    grad_zero_part, gain_one, bias_one = norm_pull_one(grad_inputs_one)
    grad_frames = grad_hidden_one + grad_zero_part
    gain_stack = jnp.stack([gain_one, gain_two, gain_three])
    bias_stack = jnp.stack([bias_one, bias_two, bias_three])
    project_share, output_share, gain_share, bias_share = (
        lax.psum_scatter(
            grad_self_project.astype(jnp.bfloat16), "shard", scatter_dimension=1, tiled=True
        ).astype(jnp.float32),
        lax.psum_scatter(
            grad_self_out.astype(jnp.bfloat16), "shard", scatter_dimension=0, tiled=True
        ).astype(jnp.float32),
        lax.psum_scatter(
            gain_stack.astype(jnp.bfloat16), "shard", scatter_dimension=1, tiled=True
        ).astype(jnp.float32),
        lax.psum_scatter(
            bias_stack.astype(jnp.bfloat16), "shard", scatter_dimension=1, tiled=True
        ).astype(jnp.float32),
    )
    summed_parts = (
        lax.psum(project_share.astype(jnp.bfloat16), "seq").astype(jnp.float32),
        lax.psum(output_share.astype(jnp.bfloat16), "seq").astype(jnp.float32),
        lax.psum(cross_share[:1].astype(jnp.bfloat16), "seq").astype(jnp.float32),
        lax.psum(cross_out_share.astype(jnp.bfloat16), "seq").astype(jnp.float32),
        lax.psum(up_share.astype(jnp.bfloat16), "seq").astype(jnp.float32),
        lax.psum(down_share.astype(jnp.bfloat16), "seq").astype(jnp.float32),
        lax.psum(gain_share.astype(jnp.bfloat16), "seq").astype(jnp.float32),
        lax.psum(bias_share.astype(jnp.bfloat16), "seq").astype(jnp.float32),
    )
    cross_final = jnp.concatenate([summed_parts[2], cross_share[1:]], axis=0)
    return (
        output,
        grad_frames,
        grad_text,
        summed_parts[6],
        summed_parts[7],
        summed_parts[0],
        summed_parts[1],
        cross_final,
        summed_parts[3],
        summed_parts[4],
        summed_parts[5],
    )


def solution(mesh):
    return jax.shard_map(
        body,
        mesh=mesh,
        in_specs=(
            P("shard", "seq", None),
            P("shard", None, None),
            P(None, "shard"),
            P(None, "shard"),
            P(None, "shard", None),
            P("shard", None),
            P(None, "shard", None),
            P("shard", None),
            P("shard", None),
            P("shard", None),
            P("shard", "seq", None),
        ),
        out_specs=(
            P("shard", "seq", None),
            P("shard", "seq", None),
            P("shard", None, None),
            P(None, "shard"),
            P(None, "shard"),
            P(None, "shard", None),
            P("shard", None),
            P(None, "shard", None),
            P("shard", None),
            P("shard", None),
            P("shard", None),
        ),
        check_vma=False,
    )
```

profile of v0, /device:TPU:0, one launch (start us, length us, event | category | flops | bytes accessed | tf_op | source)
XLA Modules:
  0.0 1739.3 jit_solution(10451731953631284153)
XLA Ops:
  11.2 10.4 all-gather
  21.7 9.2 all-gather.1
  31.7 59.6 %all-gather.9.cloned.1.call-done = bf16[3,1536,1536]{2,1,0:T(8,128)(2,1)} async-done(((bf16[3,192,1536]{2,1,0:T(8,128)(2,1)}), bf16[3,1536,1536]{2,1,0:T(8,128)(2,1)}) %all-gather.9.cloned.1.call-update) | async-done | bytes 14155792 | tf_op jit(solution)/shard_map/all_gather | solution.py:101
  91.4 9.3 fusion.27
  111.2 69.5 %all-to-all-done = bf16[3,1,256,1536]{2,0,1,3:T(4,128)(2,1)} async-done(((bf16[3,1,256,1536]{2,0,1,3:T(4,128)(2,1)}), bf16[3,1,256,1536]{2,0,1,3:T(4,128)(2,1)}, u32[]{:S(2)}, u32[]{:S(2)}) %all-to-all-start) | async-done | bytes 2359328 | tf_op jit(solution)/shard_map/all_to_all | solution.py:145
  210.0 5.5 reduce.59
  220.0 6.0 fusion.41
  228.0 11.9 all-to-all-done.1
  261.1 92.5 %all-gather.17.cloned.1.call-done = bf16[1536,6144]{1,0:T(8,128)(2,1)} async-done(((bf16[192,6144]{1,0:T(8,128)(2,1)}), bf16[1536,6144]{1,0:T(8,128)(2,1)}) %all-gather.17.cloned.1.call-update) | async-done | bytes 18874384 | tf_op jit(solution)/shard_map/all_gather | solution.py:117
  353.6 23.7 %multiply_convert_fusion.2 = (bf16[256,6144]{1,0:T(8,128)(2,1)}, f32[256,6144]{1,0:T(8,128)}, f32[256,6144]{1,0:T(8,128)}) fusion(bf16[1536,6144]{1,0:T(8,128)(2,1)} %all-gather.17.cloned.1.call-done, f32[1,256,1536]{2,1,0:T(8,128)S(1)} %get-tuple-element.192, f32[1536]{0:T(1024)S(1)} %get-tuple-element.161, f32[1536]{0:T(1024)S(1)} %get-tuple-element.206, ...), kind=kOutput, calls=%fused_computation.31 | convolution fusion | flops 4936040448 | bytes 36190208 | tf_op jit(solution)/shard_map/cfd,dk->cfk/dot_general | solution.py:23
  377.3 76.7 %all-gather.19.cloned.1.call-done = bf16[6144,1536]{1,0:T(8,128)(2,1)} async-done(((bf16[768,1536]{1,0:T(8,128)(2,1)}), bf16[6144,1536]{1,0:T(8,128)(2,1)}) %all-gather.19.cloned.1.call-update) | async-done | bytes 18874384 | tf_op jit(solution)/shard_map/all_gather | solution.py:118
  453.9 14.8 add_convert_fusion
  468.7 10.7 fusion.57
  506.5 7.0 copy.211
  513.5 24.0 %all-reduce.7.cloned.1.call-done = bf16[2,64,1536]{2,1,0:T(8,128)(2,1)} async-done(((bf16[2,64,1536]{2,1,0:T(8,128)(2,1)}), bf16[2,64,1536]{2,1,0:T(8,128)(2,1)}) %all-reduce.7.cloned.1.call-update) | async-done | bytes 393232 | tf_op jit(solution)/shard_map/psum | solution.py:212
  541.6 6.1 pad_maximum_fusion
  547.7 30.8 %copy.225 = bf16[3,1536,1536]{2,0,1:T(4,128)(2,1)} copy(bf16[3,1536,1536]{1,2,0:T(8,128)(2,1)} %pad_maximum_fusion) | data formatting | bytes 28311552
  578.5 17.0 copy.233
  607.5 8.2 reduce.60
  620.5 18.2 %all-to-all-done.2 = bf16[4,2,49152]{2,1,0:T(2,128)(2,1)S(1)} async-done(((bf16[4,2,49152]{2,1,0:T(2,128)(2,1)}), bf16[4,2,49152]{2,1,0:T(2,128)(2,1)S(1)}, u32[]{:S(2)}, u32[]{:S(2)}) %all-to-all-start.2) | async-done | bytes 786464 | tf_op jit(solution)/shard_map/all_to_all | solution.py:234
  645.1 6.2 fusion.55
  654.2 6.9 multiply_reduce_fusion.1
  661.2 6.7 multiply_convert_fusion.1
  669.3 6.8 multiply_reduce_fusion
  676.1 6.2 multiply_convert_fusion
  703.0 6.8 pad_maximum_fusion.1
  709.7 72.8 %all_to_all.60 = bf16[3,1,1024,384]{3,0,1,2:T(4,128)(2,1)S(1)} all-to-all(bf16[3,1,1024,384]{3,0,1,2:T(4,128)(2,1)S(1)} %pad_maximum_fusion.1), channel_id=1, replica_groups=mesh['seq'=4,'shard'=8] {'seq'}, dimensions={2} | all-to-all | bytes 4718592 | tf_op jit(solution)/shard_map/all_to_all | solution.py:241
  790.3 7.5 convert_bitcast_fusion
  797.7 30.8 %copy.223 = bf16[3,1536,1536]{2,0,1:T(4,128)(2,1)} copy(bf16[3,1536,1536]{1,2,0:T(8,128)(2,1)} %convert_bitcast_fusion) | data formatting | bytes 28311552
  828.6 17.0 copy.232
  846.1 5.4 convolution_convert_fusion.3
  851.6 6.0 convolution_convert_fusion.5
  858.2 12.6 convolution_convert_fusion.1
  870.9 11.4 convolution_convert_fusion
  885.5 7.4 fusion.54
  906.5 40.3 %reduce-scatter.29.cloned.1.call-done = bf16[192,4608]{1,0:T(8,128)(2,1)} async-done(((bf16[1536,4608]{1,0:T(8,128)(2,1)}), bf16[192,4608]{1,0:T(8,128)(2,1)}) %reduce-scatter.29.cloned.1.call-update) | async-done | bytes 1769488
  951.9 5.6 copy.224
  957.5 46.9 %reduce-scatter.19.cloned.1.call-done = bf16[192,1536]{1,0:T(8,128)(2,1)} async-done(((bf16[1536,1536]{1,0:T(8,128)(2,1)}), bf16[192,1536]{1,0:T(8,128)(2,1)}) %reduce-scatter.19.cloned.1.call-update) | async-done | bytes 589840 | tf_op jit(solution)/shard_map/reduce_scatter | solution.py:224
  1004.5 57.8 %reduce-scatter.17.cloned.1.call-done = bf16[192,1536]{1,0:T(8,128)(2,1)} async-done(((bf16[1536,1536]{1,0:T(8,128)(2,1)}), bf16[192,1536]{1,0:T(8,128)(2,1)}) %reduce-scatter.17.cloned.1.call-update) | async-done | bytes 589840 | tf_op jit(solution)/shard_map/reduce_scatter | solution.py:252
  1062.3 129.9 %reduce-scatter.21.cloned.1.call-done = bf16[192,6144]{1,0:T(8,128)(2,1)} async-done(((bf16[1536,6144]{1,0:T(8,128)(2,1)}), bf16[192,6144]{1,0:T(8,128)(2,1)}) %reduce-scatter.21.cloned.1.call-update) | async-done | bytes 2359312 | tf_op jit(solution)/shard_map/reduce_scatter | solution.py:189
  1192.2 130.1 %reduce-scatter.23.cloned.1.call-done = bf16[768,1536]{1,0:T(8,128)(2,1)} async-done(((bf16[6144,1536]{1,0:T(8,128)(2,1)}), bf16[768,1536]{1,0:T(8,128)(2,1)}) %reduce-scatter.23.cloned.1.call-update) | async-done | bytes 2359312 | tf_op jit(solution)/shard_map/reduce_scatter | solution.py:192
  1323.7 10.7 fusion.31
  1334.4 7.6 fusion.44
  1343.7 15.4 reduce-scatter.25.cloned.1.call-done
  1360.0 35.9 %reduce-scatter.27.cloned.1.call-done = bf16[192,3]{1,0:T(8,128)(2,1)} async-done(((bf16[1536,3]{1,0:T(8,128)(2,1)}), bf16[192,3]{1,0:T(8,128)(2,1)}) %reduce-scatter.27.cloned.1.call-update) | async-done | bytes 1168
  1396.8 11.9 all-reduce.2
  1414.7 297.1 %all-reduce.9.cloned.1.call-done = (bf16[3,192,1536]{1,2,0:T(8,128)(2,1)}, bf16[192,1536]{1,0:T(8,128)(2,1)}, bf16[1,192,1536]{1,2,0:T(8,128)(2,1)}, bf16[192,15...) async-done(((bf16[3,192,1536]{1,2,0:T(8,128)(2,1)}, bf16[192,1536]{1,0:T(8,128)(2,1)}, bf16[1,192,1536]{1,2,0:T(8,128)(2,1)}, ...) | async-done | bytes 8257552 | tf_op jit(solution)/shard_map/psum | solution.py:263
  1721.3 5.7 copy.213
  (356 shorter events, 207.0 us)
Async XLA Ops:
  7.2 212.9 %copy-start = (bf16[1,64,1536]{2,1,0:T(8,128)(2,1)S(1)}, bf16[1,64,1536]{2,1,0:T(8,128)(2,1)}, u32[]{:S(2)}) copy-start(bf16[1,64,1536]{2,1,0:T(8,128)(2,1)} %param.24) | copy-start | bytes 589828
  7.2 84.2 %all-gather.9.cloned.1.call-start = ((), (), s32[]{:S(2)}) async-start(), calls=%async_computation.12 | async-start | bytes 15925248 | tf_op jit(solution)/shard_map/all_gather | solution.py:101
  7.9 212.1 %all-gather.13.cloned.1.call-start = ((), (), s32[]{:S(2)}) async-start(), calls=%async_computation.14 | async-start | bytes 15925248 | tf_op jit(solution)/shard_map/all_gather | solution.py:110
  8.7 13.0 copy-start.90
  8.7 22.4 %copy-start.5 = (bf16[1,256,1536]{2,1,0:T(8,128)(2,1)S(1)}, bf16[1,256,1536]{2,1,0:T(8,128)(2,1)}, u32[]{:S(2)}) copy-start(bf16[1,256,1536]{2,1,0:T(8,128)(2,1)} %param.23) | copy-start | bytes 2359300
  8.7 232.6 %all-gather.11.cloned.1.call-start = ((), (), s32[]{:S(2)}) async-start(), calls=%async_computation.13 | async-start | bytes 5308416 | tf_op jit(solution)/shard_map/all_gather | solution.py:102
  9.4 247.2 %all-gather.15.cloned.1.call-start = ((), (), s32[]{:S(2)}) async-start(), calls=%async_computation.15 | async-start | bytes 5308416 | tf_op jit(solution)/shard_map/all_gather | solution.py:111
  10.0 343.6 %all-gather.17.cloned.1.call-start = ((), (), s32[]{:S(2)}) async-start(), calls=%async_computation.16 | async-start | bytes 21233664 | tf_op jit(solution)/shard_map/all_gather | solution.py:117
  10.6 443.3 %all-gather.19.cloned.1.call-start = ((), (), s32[]{:S(2)}) async-start(), calls=%async_computation.17 | async-start | bytes 21233664 | tf_op jit(solution)/shard_map/all_gather | solution.py:118
  31.1 69.6 %copy-start.54 = (f32[1536]{0:T(1024)}, f32[1536]{0:T(1024)S(1)}, u32[]{:S(2)}) copy-start(f32[1536]{0:T(1024)S(1)} %get-tuple-element.204) | copy-start | bytes 18436
  31.1 69.6 %copy-start.65 = (f32[1536]{0:T(1024)}, f32[1536]{0:T(1024)S(1)}, u32[]{:S(2)}) copy-start(f32[1536]{0:T(1024)S(1)} %get-tuple-element.163) | copy-start | bytes 18436
  31.1 214.7 %copy-start.67 = (f32[1536]{0:T(1024)}, f32[1536]{0:T(1024)S(1)}, u32[]{:S(2)}) copy-start(f32[1536]{0:T(1024)S(1)} %get-tuple-element.205) | copy-start | bytes 18436
  31.1 214.7 %copy-start.83 = (f32[1536]{0:T(1024)}, f32[1536]{0:T(1024)S(1)}, u32[]{:S(2)}) copy-start(f32[1536]{0:T(1024)S(1)} %get-tuple-element.162) | copy-start | bytes 18436
  31.1 322.4 %copy-start.56 = (f32[1536]{0:T(1024)}, f32[1536]{0:T(1024)S(1)}, u32[]{:S(2)}) copy-start(f32[1536]{0:T(1024)S(1)} %get-tuple-element.161) | copy-start | bytes 18436
  31.4 69.4 %copy-start.70 = (f32[256]{0:T(256)}, f32[256]{0:T(256)S(1)}, u32[]{:S(2)}) copy-start(f32[256]{0:T(256)S(1)} %broadcast_multiply_fusion.2) | copy-start | bytes 3076
  31.7 69.0 %copy-start.76 = (f32[256]{0:T(256)}, f32[256]{0:T(256)S(1)}, u32[]{:S(2)}) copy-start(f32[256]{0:T(256)S(1)} %fusion.53) | copy-start | bytes 3076
  31.7 69.0 %copy-start.72 = (f32[256]{0:T(256)}, f32[256]{0:T(256)S(1)}, u32[]{:S(2)}) copy-start(f32[256]{0:T(256)S(1)} %fusion.100) | copy-start | bytes 3076
  104.3 76.4 %all-to-all-start = ((bf16[3,1,256,1536]{2,0,1,3:T(4,128)(2,1)}), bf16[3,1,256,1536]{2,0,1,3:T(4,128)(2,1)}, u32[]{:S(2)}, u32[]{:S(2)}) async-start(bf16[3,1,256,1536]{2,0,1,3:T(4,128)(2,1)} %copy.187), calls=%async_computation | async-start | bytes 6291456 | tf_op jit(solution)/shard_map/all_to_all | solution.py:145
  187.2 8.9 copy-start.25
  189.2 14.4 copy-start.35
  216.4 23.5 %all-to-all-start.1 = ((bf16[4,2,49152]{2,1,0:T(2,128)(2,1)}), bf16[4,2,49152]{2,1,0:T(2,128)(2,1)S(1)}, u32[]{:S(2)}, u32[]{:S(2)}) async-start(bf16[4,2,49152]{2,1,0:T(2,128)(2,1)} %reshape.954), calls=%async_computation.1 | async-start | bytes 1572864 | tf_op jit(solution)/shard_map/all_to_all | solution.py:150
  220.0 317.6 %all-reduce.7.cloned.1.call-start = ((), (), s32[]{:S(2)}) async-start(), calls=%async_computation.18 | async-start | bytes 786432 | tf_op jit(solution)/shard_map/psum | solution.py:212
  254.0 237.8 %copy-start.58 = (f32[24,256]{1,0:T(8,128)}, f32[24,256]{1,0:T(8,128)S(1)}, u32[]{:S(2)}) copy-start(f32[24,256]{1,0:T(8,128)S(1)} %get-tuple-element.189) | copy-start | bytes 73732
  260.8 218.7 %copy-start.9 = (f32[1,256,1536]{2,1,0:T(8,128)}, f32[1,256,1536]{2,1,0:T(8,128)S(1)}, u32[]{:S(2)}) copy-start(f32[1,256,1536]{2,1,0:T(8,128)S(1)} %get-tuple-element.192) | copy-start | bytes 4718596
  500.4 396.8 %reduce-scatter.31.cloned.1.call-start = ((), (), s32[]{:S(2)}) async-start(), calls=%async_computation.26 | async-start | bytes 15925248
  595.6 9.2 slice-start.3
  596.7 8.1 slice-start.4
  607.4 13.0 copy-start.60
  607.5 13.0 copy-start.62
  607.5 13.0 copy-start.53
  607.5 13.0 copy-start.64
  616.7 22.0 %all-to-all-start.2 = ((bf16[4,2,49152]{2,1,0:T(2,128)(2,1)}), bf16[4,2,49152]{2,1,0:T(2,128)(2,1)S(1)}, u32[]{:S(2)}, u32[]{:S(2)}) async-start(bf16[4,2,49152]{2,1,0:T(2,128)(2,1)} %reshape.956), calls=%async_computation.2 | async-start | bytes 1572864 | tf_op jit(solution)/shard_map/all_to_all | solution.py:234
  620.5 326.3 %reduce-scatter.29.cloned.1.call-start = ((), (), s32[]{:S(2)}) async-start(), calls=%async_computation.25 | async-start | bytes 15925248
  641.0 13.3 copy-start.21
  645.1 9.1 copy-start.42
  654.2 14.7 slice-start
  654.2 14.7 slice-start.1
  661.2 7.8 slice-start.2
  845.6 158.8 %reduce-scatter.19.cloned.1.call-start = ((), (), s32[]{:S(2)}) async-start(), calls=%async_computation.20 | async-start | bytes 5308416 | tf_op jit(solution)/shard_map/reduce_scatter | solution.py:224
  851.5 210.8 %reduce-scatter.17.cloned.1.call-start = ((), (), s32[]{:S(2)}) async-start(), calls=%async_computation.19 | async-start | bytes 5308416 | tf_op jit(solution)/shard_map/reduce_scatter | solution.py:252
  857.6 334.7 %reduce-scatter.21.cloned.1.call-start = ((), (), s32[]{:S(2)}) async-start(), calls=%async_computation.21 | async-start | bytes 21233664 | tf_op jit(solution)/shard_map/reduce_scatter | solution.py:189
  870.8 451.5 %reduce-scatter.23.cloned.1.call-start = ((), (), s32[]{:S(2)}) async-start(), calls=%async_computation.22 | async-start | bytes 21233664 | tf_op jit(solution)/shard_map/reduce_scatter | solution.py:192
  882.3 476.8 %reduce-scatter.25.cloned.1.call-start = ((), (), s32[]{:S(2)}) async-start(), calls=%async_computation.23 | async-start | bytes 442368
  895.9 500.1 %reduce-scatter.27.cloned.1.call-start = ((), (), s32[]{:S(2)}) async-start(), calls=%async_computation.24 | async-start | bytes 442368
  897.0 814.8 %all-reduce.9.cloned.1.call-start = ((), (), s32[]{:S(2)}) async-start(), calls=%async_computation.27 | async-start | bytes 18087936 | tf_op jit(solution)/shard_map/psum | solution.py:263
  901.0 50.9 %copy-start.17 = (bf16[192,3,1536]{2,1,0:T(4,128)(2,1)}, bf16[192,3,1536]{2,1,0:T(4,128)(2,1)S(1)}, u32[]{:S(2)}) copy-start(bf16[192,3,1536]{2,1,0:T(4,128)(2,1)S(1)} %reshape.947) | copy-start | bytes 5308420
  1323.7 10.7 copy-start.43
  1342.0 67.9 %copy-start.18 = (bf16[192,3,1536]{2,1,0:T(4,128)(2,1)S(1)}, bf16[192,3,1536]{2,1,0:T(4,128)(2,1)}, u32[]{:S(2)}) copy-start(bf16[192,3,1536]{2,1,0:T(4,128)(2,1)} %copy-done.17) | copy-start | bytes 5308420
  (67 other events, 242.5 us)
Sparse Core Ops, SparseCore 0:
  9.9 81.4 all-gather.8
  93.3 78.6 all-gather.12
  173.8 38.7 all-gather.10
  214.4 38.7 all-gather.14
  255.0 98.5 all-gather.16
  355.3 98.5 all-gather.18
  500.6 36.9 all-reduce.6
  595.7 101.5 reduce-scatter.30
  845.8 100.9 reduce-scatter.28
  950.6 53.7 reduce-scatter.18
  1008.5 53.7 reduce-scatter.16
  1065.8 126.4 reduce-scatter.20
  1195.8 126.4 reduce-scatter.22
  1325.2 33.8 reduce-scatter.24
  1362.0 33.8 reduce-scatter.26
  1399.6 312.1 all-reduce.8
where the time goes:
time: 1750 us; the launch traced here: 1740 us
  waiting for transfers between devices  1110 us (63%)
  matrix products  220 us (13%)
  local copies, waits for them, and re-layouts  207 us (12%)
  blocking collectives  104 us (6%)
  other arithmetic  70.1 us (4%)
    psum x1, waiting for transfers between devices, body(): lax.psum(project_share.astype(jnp.bfloat16), 'seq').astype(jnp.float32)  297 us
    dot_general x38, matrix products, contract(): return jnp.einsum(form, left, right, preferred_element_type=jnp.float32)  218 us
    unnamed x214, local copies, waits for them, and re-layouts  146 us
    reduce_scatter x1, waiting for transfers between devices, body(): lax.psum_scatter(grad_down.astype(jnp.bfloat16), 'shard', scatter_dimensi...  130 us
    reduce_scatter x1, waiting for transfers between devices, body(): lax.psum_scatter(grad_up.astype(jnp.bfloat16), 'shard', scatter_dimension...  130 us
    unnamed x20, waiting for transfers between devices  95.5 us
    all_gather x1, waiting for transfers between devices, fetch_mlp(): lax.all_gather(up_weight, 'shard', axis=0, tiled=True)  92.5 us
    all_gather x1, waiting for transfers between devices, fetch_mlp(): lax.all_gather(down_weight, 'shard', axis=0, tiled=True)  76.7 us
  transfers between devices with their start and end apart: 19, of which 15 were waited for; matrix products, arithmetic and copies ran while one was open for 21% of the time, Pallas kernels for 0%

commit v1 on v0

--- a/solution.py
+++ b/solution.py
@@ -7,6 +7,18 @@
 QBLOCK = 512
 EPSILON = 1e-05
 MASKED_SCORE = -1e30
+
+
+def split_up(x, dim, length):
+    shape = x.shape
+    parts = x.reshape(*shape[:dim], length, shape[dim] // length, *shape[dim + 1 :])
+    return jnp.moveaxis(parts, dim, 0)
+
+
+def joined_along(parts, dim):
+    parts = jnp.moveaxis(parts, 0, dim)
+    shape = parts.shape
+    return parts.reshape(*shape[:dim], shape[dim] * shape[dim + 1], *shape[dim + 2 :])
 
 
 def layer_norm(hidden, gain, shift):
@@ -142,7 +154,14 @@
     normed_one, norm_pull_one = jax.vjp(layer_norm, hidden, gains[0], biases[0])
     inputs_one = normed_one.astype(jnp.bfloat16)
     projected = contract("cfd,jde->jcfe", inputs_one, project_all).astype(jnp.bfloat16)
-    by_heads = lax.all_to_all(projected, "seq", split_axis=3, concat_axis=2, tiled=True)
+    size, place = (lax.axis_size("seq"), lax.axis_index("seq"))
+    blocks = split_up(projected, 3, size)
+    outs = [blocks[place]]
+    for lap in range(1, size):
+        sent = blocks[(place + lap) % size]
+        outs.append(lax.ppermute(sent, "seq", [(i, (i + lap) % size) for i in range(size)]))
+    blocks = jnp.stack(outs)[(place - jnp.arange(size)) % size]
+    by_heads = joined_along(blocks, 2)
     queries = split_heads(by_heads[0])
     key_rows = split_heads(by_heads[1])
     value_rows = split_heads(by_heads[2])

time: 1750 us -> 1750 us (level)
    all_to_all x1 -> x0, waiting for transfers between devices: 69.5 us -> none  [body(): lax.all_to_all(projected, 'seq', split_axis=3, concat_axis=2, tiled=True)]
    ppermute x0 -> x3, waiting for transfers between devices: none -> 47.8 us  [body(): lax.ppermute(sent, 'seq', [(i, (i + lap) % size) for i in range(size)])]
    unnamed x214 -> x218, local copies, waits for them, and re-layouts: 146 us -> 147 us
  transfers between devices with their start and end apart: 19 -> 21, of which waited for: 15 -> 18; matrix products, arithmetic and copies ran while one was open for 21% -> 21% of each run, Pallas kernels for 0% -> 0%
where the time goes in v1:
time: 1750 us; the launch traced here: 1740 us
  waiting for transfers between devices  1100 us (63%)
  matrix products  221 us (13%)
  local copies, waits for them, and re-layouts  217 us (12%)
  blocking collectives  104 us (6%)
  other arithmetic  69.8 us (4%)
    psum x1, waiting for transfers between devices, body(): lax.psum(project_share.astype(jnp.bfloat16), 'seq').astype(jnp.float32)  297 us
    dot_general x38, matrix products, contract(): return jnp.einsum(form, left, right, preferred_element_type=jnp.float32)  219 us
    unnamed x218, local copies, waits for them, and re-layouts  147 us
    reduce_scatter x1, waiting for transfers between devices, body(): lax.psum_scatter(grad_down.astype(jnp.bfloat16), 'shard', scatter_dimensi...  130 us
    reduce_scatter x1, waiting for transfers between devices, body(): lax.psum_scatter(grad_up.astype(jnp.bfloat16), 'shard', scatter_dimension...  130 us
    all_gather x1, waiting for transfers between devices, fetch_mlp(): lax.all_gather(up_weight, 'shard', axis=0, tiled=True)  96 us
    unnamed x20, waiting for transfers between devices  95.6 us
    all_gather x1, waiting for transfers between devices, fetch_mlp(): lax.all_gather(down_weight, 'shard', axis=0, tiled=True)  76.7 us
  transfers between devices with their start and end apart: 21, of which 18 were waited for; matrix products, arithmetic and copies ran while one was open for 21% of the time, Pallas kernels for 0%

profile of v1, /device:TPU:0, one launch (start us, length us, event | category | flops | bytes accessed | tf_op | source)
XLA Modules:
  0.0 1739.8 jit_solution(7159831616085723785)
XLA Ops:
  11.2 10.4 all-gather
  21.7 9.2 all-gather.1
  31.8 59.6 %all-gather.9.cloned.1.call-done = bf16[3,1536,1536]{2,1,0:T(8,128)(2,1)} async-done(((bf16[3,192,1536]{2,1,0:T(8,128)(2,1)}), bf16[3,1536,1536]{2,1,0:T(8,128)(2,1)}) %all-gather.9.cloned.1.call-update) | async-done | bytes 14155792 | tf_op jit(solution)/shard_map/all_gather | solution.py:113
  91.4 10.3 fusion.27
  118.2 10.6 collective-permute-done.2
  128.8 13.7 collective-permute-done
  142.5 23.5 %collective-permute-done.1 = bf16[3,1,256,384]{3,2,0,1:T(8,128)(2,1)S(1)} collective-permute-done((bf16[3,1,256,384]{3,2,0,1:T(8,128)(2,1)S(1)}, bf16[3,1,256,384]{3,2,0,1:T(8,128)(2,1)S(1)}, u32[]{:S(2)}, u32[]{:S(2)}) %collective-permute-start.1) | collective-permute-done | bytes 589856 | tf_op jit(solution)/shard_map/ppermute | solution.py:162
  216.9 12.0 all-to-all-done
  245.7 7.5 all-gather.15.cloned.1.call-done
  257.6 96.0 %all-gather.17.cloned.1.call-done = bf16[1536,6144]{1,0:T(8,128)(2,1)} async-done(((bf16[192,6144]{1,0:T(8,128)(2,1)}), bf16[1536,6144]{1,0:T(8,128)(2,1)}) %all-gather.17.cloned.1.call-update) | async-done | bytes 18874384 | tf_op jit(solution)/shard_map/all_gather | solution.py:129
  353.6 23.7 %multiply_convert_fusion.2 = (bf16[256,6144]{1,0:T(8,128)(2,1)}, f32[256,6144]{1,0:T(8,128)}, f32[256,6144]{1,0:T(8,128)}) fusion(bf16[1536,6144]{1,0:T(8,128)(2,1)} %all-gather.17.cloned.1.call-done, f32[1,256,1536]{2,1,0:T(8,128)S(1)} %get-tuple-element.196, f32[1536]{0:T(1024)S(1)} %get-tuple-element.161, f32[1536]{0:T(1024)S(1)} %get-tuple-element.210, ...), kind=kOutput, calls=%fused_computation.32 | convolution fusion | flops 4936040448 | bytes 36190208 | tf_op jit(solution)/shard_map/cfd,dk->cfk/dot_general | solution.py:35
  377.3 76.7 %all-gather.19.cloned.1.call-done = bf16[6144,1536]{1,0:T(8,128)(2,1)} async-done(((bf16[768,1536]{1,0:T(8,128)(2,1)}), bf16[6144,1536]{1,0:T(8,128)(2,1)}) %all-gather.19.cloned.1.call-update) | async-done | bytes 18874384 | tf_op jit(solution)/shard_map/all_gather | solution.py:130
  453.9 15.0 add_convert_fusion
  468.9 10.7 fusion.57
  506.7 6.8 copy.248
  513.5 24.3 %all-reduce.7.cloned.1.call-done = bf16[2,64,1536]{2,1,0:T(8,128)(2,1)} async-done(((bf16[2,64,1536]{2,1,0:T(8,128)(2,1)}), bf16[2,64,1536]{2,1,0:T(8,128)(2,1)}) %all-reduce.7.cloned.1.call-update) | async-done | bytes 393232 | tf_op jit(solution)/shard_map/psum | solution.py:231
  541.8 6.1 pad_maximum_fusion
  547.9 31.0 %copy.262 = bf16[3,1536,1536]{2,0,1:T(4,128)(2,1)} copy(bf16[3,1536,1536]{1,2,0:T(8,128)(2,1)} %pad_maximum_fusion) | data formatting | bytes 28311552
  578.8 17.0 copy.274
  607.8 8.2 reduce.60
  620.8 18.2 %all-to-all-done.1 = bf16[4,2,49152]{2,1,0:T(2,128)(2,1)S(1)} async-done(((bf16[4,2,49152]{2,1,0:T(2,128)(2,1)}), bf16[4,2,49152]{2,1,0:T(2,128)(2,1)S(1)}, u32[]{:S(2)}, u32[]{:S(2)}) %all-to-all-start.1) | async-done | bytes 786464 | tf_op jit(solution)/shard_map/all_to_all | solution.py:253
  645.4 6.2 fusion.55
  654.5 6.9 multiply_reduce_fusion.1
  661.5 6.7 multiply_convert_fusion.1
  669.7 6.8 multiply_reduce_fusion
  676.5 6.2 multiply_convert_fusion
  703.4 6.8 pad_maximum_fusion.1
  710.2 72.8 %all_to_all.45 = bf16[3,1,1024,384]{3,0,1,2:T(4,128)(2,1)S(1)} all-to-all(bf16[3,1,1024,384]{3,0,1,2:T(4,128)(2,1)S(1)} %pad_maximum_fusion.1), channel_id=1, replica_groups=mesh['seq'=4,'shard'=8] {'seq'}, dimensions={2} | all-to-all | bytes 4718592 | tf_op jit(solution)/shard_map/all_to_all | solution.py:260
  790.7 7.3 convert_bitcast_fusion
  798.0 31.0 %copy.260 = bf16[3,1536,1536]{2,0,1:T(4,128)(2,1)} copy(bf16[3,1536,1536]{1,2,0:T(8,128)(2,1)} %convert_bitcast_fusion) | data formatting | bytes 28311552
  828.9 17.0 copy.273
  851.4 6.2 convolution_convert_fusion.5
  858.4 12.8 convolution_convert_fusion.1
  871.3 11.4 convolution_convert_fusion
  885.8 7.4 fusion.54
  906.9 40.3 %reduce-scatter.29.cloned.1.call-done = bf16[192,4608]{1,0:T(8,128)(2,1)} async-done(((bf16[1536,4608]{1,0:T(8,128)(2,1)}), bf16[192,4608]{1,0:T(8,128)(2,1)}) %reduce-scatter.29.cloned.1.call-update) | async-done | bytes 1769488
  952.4 5.6 copy.261
  958.0 46.9 %reduce-scatter.19.cloned.1.call-done = bf16[192,1536]{1,0:T(8,128)(2,1)} async-done(((bf16[1536,1536]{1,0:T(8,128)(2,1)}), bf16[192,1536]{1,0:T(8,128)(2,1)}) %reduce-scatter.19.cloned.1.call-update) | async-done | bytes 589840 | tf_op jit(solution)/shard_map/reduce_scatter | solution.py:243
  1004.9 57.8 %reduce-scatter.17.cloned.1.call-done = bf16[192,1536]{1,0:T(8,128)(2,1)} async-done(((bf16[1536,1536]{1,0:T(8,128)(2,1)}), bf16[192,1536]{1,0:T(8,128)(2,1)}) %reduce-scatter.17.cloned.1.call-update) | async-done | bytes 589840 | tf_op jit(solution)/shard_map/reduce_scatter | solution.py:271
  1062.7 129.9 %reduce-scatter.21.cloned.1.call-done = bf16[192,6144]{1,0:T(8,128)(2,1)} async-done(((bf16[1536,6144]{1,0:T(8,128)(2,1)}), bf16[192,6144]{1,0:T(8,128)(2,1)}) %reduce-scatter.21.cloned.1.call-update) | async-done | bytes 2359312 | tf_op jit(solution)/shard_map/reduce_scatter | solution.py:208
  1192.7 130.1 %reduce-scatter.23.cloned.1.call-done = bf16[768,1536]{1,0:T(8,128)(2,1)} async-done(((bf16[6144,1536]{1,0:T(8,128)(2,1)}), bf16[768,1536]{1,0:T(8,128)(2,1)}) %reduce-scatter.23.cloned.1.call-update) | async-done | bytes 2359312 | tf_op jit(solution)/shard_map/reduce_scatter | solution.py:211
  1324.2 10.7 fusion.31
  1334.9 7.6 fusion.44
  1344.2 15.4 reduce-scatter.25.cloned.1.call-done
  1360.5 36.0 %reduce-scatter.27.cloned.1.call-done = bf16[192,3]{1,0:T(8,128)(2,1)} async-done(((bf16[1536,3]{1,0:T(8,128)(2,1)}), bf16[192,3]{1,0:T(8,128)(2,1)}) %reduce-scatter.27.cloned.1.call-update) | async-done | bytes 1168
  1397.3 11.9 all-reduce.2
  1415.2 297.1 %all-reduce.9.cloned.1.call-done = (bf16[3,192,1536]{1,2,0:T(8,128)(2,1)}, bf16[192,1536]{1,0:T(8,128)(2,1)}, bf16[1,192,1536]{1,2,0:T(8,128)(2,1)}, bf16[192,15...) async-done(((bf16[3,192,1536]{1,2,0:T(8,128)(2,1)}, bf16[192,1536]{1,0:T(8,128)(2,1)}, bf16[1,192,1536]{1,2,0:T(8,128)(2,1)}, ...) | async-done | bytes 8257552 | tf_op jit(solution)/shard_map/psum | solution.py:282
  1721.8 5.7 copy.250
  (371 shorter events, 233.3 us)
Async XLA Ops:
  7.2 202.2 %copy-start = (bf16[1,64,1536]{2,1,0:T(8,128)(2,1)S(1)}, bf16[1,64,1536]{2,1,0:T(8,128)(2,1)}, u32[]{:S(2)}) copy-start(bf16[1,64,1536]{2,1,0:T(8,128)(2,1)} %param.24) | copy-start | bytes 589828
  7.2 84.2 %all-gather.9.cloned.1.call-start = ((), (), s32[]{:S(2)}) async-start(), calls=%async_computation.11 | async-start | bytes 15925248 | tf_op jit(solution)/shard_map/all_gather | solution.py:113
  7.9 201.5 %all-gather.13.cloned.1.call-start = ((), (), s32[]{:S(2)}) async-start(), calls=%async_computation.13 | async-start | bytes 15925248 | tf_op jit(solution)/shard_map/all_gather | solution.py:122
  8.7 13.0 copy-start.90
  8.7 22.4 %copy-start.5 = (bf16[1,256,1536]{2,1,0:T(8,128)(2,1)S(1)}, bf16[1,256,1536]{2,1,0:T(8,128)(2,1)}, u32[]{:S(2)}) copy-start(bf16[1,256,1536]{2,1,0:T(8,128)(2,1)} %param.23) | copy-start | bytes 2359300
  8.7 221.6 %all-gather.11.cloned.1.call-start = ((), (), s32[]{:S(2)}) async-start(), calls=%async_computation.12 | async-start | bytes 5308416 | tf_op jit(solution)/shard_map/all_gather | solution.py:114
  9.4 243.8 %all-gather.15.cloned.1.call-start = ((), (), s32[]{:S(2)}) async-start(), calls=%async_computation.14 | async-start | bytes 5308416 | tf_op jit(solution)/shard_map/all_gather | solution.py:123
  10.0 343.6 %all-gather.17.cloned.1.call-start = ((), (), s32[]{:S(2)}) async-start(), calls=%async_computation.15 | async-start | bytes 21233664 | tf_op jit(solution)/shard_map/all_gather | solution.py:129
  10.6 443.3 %all-gather.19.cloned.1.call-start = ((), (), s32[]{:S(2)}) async-start(), calls=%async_computation.16 | async-start | bytes 21233664 | tf_op jit(solution)/shard_map/all_gather | solution.py:130
  31.1 60.2 %copy-start.54 = (f32[1536]{0:T(1024)}, f32[1536]{0:T(1024)S(1)}, u32[]{:S(2)}) copy-start(f32[1536]{0:T(1024)S(1)} %get-tuple-element.208) | copy-start | bytes 18436
  31.2 70.5 %copy-start.65 = (f32[1536]{0:T(1024)}, f32[1536]{0:T(1024)S(1)}, u32[]{:S(2)}) copy-start(f32[1536]{0:T(1024)S(1)} %get-tuple-element.163) | copy-start | bytes 18436
  31.2 203.6 %copy-start.67 = (f32[1536]{0:T(1024)}, f32[1536]{0:T(1024)S(1)}, u32[]{:S(2)}) copy-start(f32[1536]{0:T(1024)S(1)} %get-tuple-element.209) | copy-start | bytes 18436
  31.2 203.6 %copy-start.83 = (f32[1536]{0:T(1024)}, f32[1536]{0:T(1024)S(1)}, u32[]{:S(2)}) copy-start(f32[1536]{0:T(1024)S(1)} %get-tuple-element.162) | copy-start | bytes 18436
  31.2 322.4 %copy-start.56 = (f32[1536]{0:T(1024)}, f32[1536]{0:T(1024)S(1)}, u32[]{:S(2)}) copy-start(f32[1536]{0:T(1024)S(1)} %get-tuple-element.161) | copy-start | bytes 18436
  31.4 70.3 %copy-start.70 = (f32[256]{0:T(256)}, f32[256]{0:T(256)S(1)}, u32[]{:S(2)}) copy-start(f32[256]{0:T(256)S(1)} %broadcast_multiply_fusion.2) | copy-start | bytes 3076
  31.8 70.0 %copy-start.76 = (f32[256]{0:T(256)}, f32[256]{0:T(256)S(1)}, u32[]{:S(2)}) copy-start(f32[256]{0:T(256)S(1)} %fusion.53) | copy-start | bytes 3076
  31.8 69.9 %copy-start.72 = (f32[256]{0:T(256)}, f32[256]{0:T(256)S(1)}, u32[]{:S(2)}) copy-start(f32[256]{0:T(256)S(1)} %fusion.100) | copy-start | bytes 3076
  111.7 17.1 collective-permute-start.2
  115.1 27.5 %collective-permute-start = (bf16[3,1,256,384]{3,2,0,1:T(8,128)(2,1)S(1)}, bf16[3,1,256,384]{3,2,0,1:T(8,128)(2,1)S(1)}, u32[]{:S(2)}, u32[]{:S(2)}) collective-permute-start(bf16[3,1,256,384]{3,2,0,1:T(8,128)(2,1)S(1)} %bitcast.393), channel_id=1, source_target_pairs={{0,8},{8,16},{16,24},{24,0},{1,9},{9,17},{17,25},{25,1},{2,10},{10... | collective-permute-start | bytes 1769480 | tf_op jit(solution)/shard_map/ppermute | solution.py:162
  115.1 51.0 %collective-permute-start.1 = (bf16[3,1,256,384]{3,2,0,1:T(8,128)(2,1)S(1)}, bf16[3,1,256,384]{3,2,0,1:T(8,128)(2,1)S(1)}, u32[]{:S(2)}, u32[]{:S(2)}) collective-permute-start(bf16[3,1,256,384]{3,2,0,1:T(8,128)(2,1)S(1)} %bitcast.392), channel_id=1, source_target_pairs={{0,16},{8,24},{16,0},{24,8},{1,17},{9,25},{17,1},{25,9},{2,18},{10... | collective-permute-start | bytes 1769480 | tf_op jit(solution)/shard_map/ppermute | solution.py:162
  173.3 11.9 copy-start.25
  176.1 16.2 copy-start.35
  205.5 23.3 %all-to-all-start = ((bf16[4,2,49152]{2,1,0:T(2,128)(2,1)}), bf16[4,2,49152]{2,1,0:T(2,128)(2,1)S(1)}, u32[]{:S(2)}, u32[]{:S(2)}) async-start(bf16[4,2,49152]{2,1,0:T(2,128)(2,1)} %reshape.1025), calls=%async_computation | async-start | bytes 1572864 | tf_op jit(solution)/shard_map/all_to_all | solution.py:169
  209.4 328.4 %all-reduce.7.cloned.1.call-start = ((), (), s32[]{:S(2)}) async-start(), calls=%async_computation.17 | async-start | bytes 786432 | tf_op jit(solution)/shard_map/psum | solution.py:231
  243.0 249.0 %copy-start.58 = (f32[24,256]{1,0:T(8,128)}, f32[24,256]{1,0:T(8,128)S(1)}, u32[]{:S(2)}) copy-start(f32[24,256]{1,0:T(8,128)S(1)} %get-tuple-element.193) | copy-start | bytes 73732
  257.3 222.4 %copy-start.9 = (f32[1,256,1536]{2,1,0:T(8,128)}, f32[1,256,1536]{2,1,0:T(8,128)S(1)}, u32[]{:S(2)}) copy-start(f32[1,256,1536]{2,1,0:T(8,128)S(1)} %get-tuple-element.196) | copy-start | bytes 4718596
  500.7 397.0 %reduce-scatter.31.cloned.1.call-start = ((), (), s32[]{:S(2)}) async-start(), calls=%async_computation.25 | async-start | bytes 15925248
  595.9 9.2 slice-start.3
  607.8 13.0 copy-start.60
  607.8 13.0 copy-start.62
  607.8 13.0 copy-start.53
  607.8 13.0 copy-start.64
  617.0 22.0 %all-to-all-start.1 = ((bf16[4,2,49152]{2,1,0:T(2,128)(2,1)}), bf16[4,2,49152]{2,1,0:T(2,128)(2,1)S(1)}, u32[]{:S(2)}, u32[]{:S(2)}) async-start(bf16[4,2,49152]{2,1,0:T(2,128)(2,1)} %reshape.1027), calls=%async_computation.1 | async-start | bytes 1572864 | tf_op jit(solution)/shard_map/all_to_all | solution.py:253
  620.7 326.5 %reduce-scatter.29.cloned.1.call-start = ((), (), s32[]{:S(2)}) async-start(), calls=%async_computation.24 | async-start | bytes 15925248
  641.2 13.3 copy-start.21
  645.4 9.1 copy-start.42
  654.5 14.7 slice-start
  654.5 14.7 slice-start.1
  846.0 158.9 %reduce-scatter.19.cloned.1.call-start = ((), (), s32[]{:S(2)}) async-start(), calls=%async_computation.19 | async-start | bytes 5308416 | tf_op jit(solution)/shard_map/reduce_scatter | solution.py:243
  851.3 211.4 %reduce-scatter.17.cloned.1.call-start = ((), (), s32[]{:S(2)}) async-start(), calls=%async_computation.18 | async-start | bytes 5308416 | tf_op jit(solution)/shard_map/reduce_scatter | solution.py:271
  857.7 335.0 %reduce-scatter.21.cloned.1.call-start = ((), (), s32[]{:S(2)}) async-start(), calls=%async_computation.20 | async-start | bytes 21233664 | tf_op jit(solution)/shard_map/reduce_scatter | solution.py:208
  871.2 451.5 %reduce-scatter.23.cloned.1.call-start = ((), (), s32[]{:S(2)}) async-start(), calls=%async_computation.21 | async-start | bytes 21233664 | tf_op jit(solution)/shard_map/reduce_scatter | solution.py:211
  882.7 476.9 %reduce-scatter.25.cloned.1.call-start = ((), (), s32[]{:S(2)}) async-start(), calls=%async_computation.22 | async-start | bytes 442368
  896.3 500.2 %reduce-scatter.27.cloned.1.call-start = ((), (), s32[]{:S(2)}) async-start(), calls=%async_computation.23 | async-start | bytes 442368
  897.4 814.9 %all-reduce.9.cloned.1.call-start = ((), (), s32[]{:S(2)}) async-start(), calls=%async_computation.26 | async-start | bytes 18087936 | tf_op jit(solution)/shard_map/psum | solution.py:282
  901.4 51.0 %copy-start.17 = (bf16[192,3,1536]{2,1,0:T(4,128)(2,1)}, bf16[192,3,1536]{2,1,0:T(4,128)(2,1)S(1)}, u32[]{:S(2)}) copy-start(bf16[192,3,1536]{2,1,0:T(4,128)(2,1)S(1)} %reshape.1018) | copy-start | bytes 5308420
  1324.2 10.7 copy-start.43
  1342.5 67.9 %copy-start.18 = (bf16[192,3,1536]{2,1,0:T(4,128)(2,1)S(1)}, bf16[192,3,1536]{2,1,0:T(4,128)(2,1)}, u32[]{:S(2)}) copy-start(bf16[192,3,1536]{2,1,0:T(4,128)(2,1)} %copy-done.17) | copy-start | bytes 5308420
  (69 other events, 257.2 us)
Sparse Core Ops, SparseCore 0:
  9.9 81.4 all-gather.8
  93.3 78.6 all-gather.12
  173.8 38.7 all-gather.10
  214.4 38.7 all-gather.14
  254.9 98.5 all-gather.16
  355.3 98.5 all-gather.18
  500.8 36.9 all-reduce.6
  596.0 101.5 reduce-scatter.30
  846.1 101.0 reduce-scatter.28
  951.1 53.7 reduce-scatter.18
  1008.9 53.7 reduce-scatter.16
  1066.2 126.4 reduce-scatter.20
  1196.3 126.4 reduce-scatter.22
  1325.7 33.8 reduce-scatter.24
  1362.5 33.8 reduce-scatter.26
  1400.1 312.1 all-reduce.8
